TPU v7x, 128 devices: a whole 4x4x4 slice. The times are simulated.
128 devices in a mesh: req: 16 (over y, z), mdl: 8 (over x, core).
Axes of the slice: x: 4, y: 4, z: 4, core: 2. Of those that a mesh axis runs over, the one named last changes fastest.
Arguments:
- segments: int32 [1024], P('req'), may hold values from -1 to 1023, as said below
- queries: bfloat16 [1024, 8192], P('req', 'mdl'), may hold values from -200 to 200
- keys_values: bfloat16 [1024, 2, 1024], P('req', None, 'mdl'), may hold values from -6 to 6
- page_table: int32 [64], replicated, may hold values from 0 to 127, as said below
- paged_cache: bfloat16 [128, 16, 2, 1024], P('req', None, None, 'mdl'), may hold values from -6 to 6
- residual: bfloat16 [1024, 8192], P(None, 'req'), may hold values from -40 to 40
- out_weight: bfloat16 [8192, 8192], P('mdl', 'req'), may hold values from -0.0625 to 0.0625
- norm_gain: bfloat16 [8192], P('req'), may hold values from 0.099609375 to 1.8984375
- gate_up_weight: bfloat16 [8192, 2, 29568], P('req', None, 'mdl'), may hold values from -0.0625 to 0.0625
Outputs:
- hidden: bfloat16 [1024, 29568], P('req', 'mdl')
- cache_new: bfloat16 [128, 16, 2, 1024], P('req', None, None, 'mdl')
Inputs may be any that keep to these rules, and one draw needn't show every extreme that they name: `segments`: each block of 64 slots of one index of req holds whole requests followed by pads; a live slot's entry is the slot index of its request's first slot, in that block; in every draw some block has no pads. `page_table`: all entries differ; page p lies on index p // 8 of req; the pages of one block of 64 slots all lie on one index of req, and different blocks on different indices.
All inputs are finite; a program needn't handle non-finite values.
Results may differ from a plain program's by a relative error of at most 0.024.
Values may be sent and summed in bfloat16 or wider, within the bound.
A program may use at most 128 MiB of HBM per device.

v0:
```python
import jax
import jax.numpy as jnp
from jax import lax
from jax.sharding import PartitionSpec as P

D = 8192
HD = 128
QPK = 8
PAGE = 16
EPSILON = 1e-06


def attention_block(query_rows, pair_rows, seg_rows):
    slots = seg_rows.shape[0]
    groups = pair_rows.shape[2] // HD
    query = query_rows.reshape(slots, groups, QPK, HD)
    keys = pair_rows[:, 0].reshape(slots, groups, HD)
    values = pair_rows[:, 1].reshape(slots, groups, HD)
    scores = jnp.einsum("igqd,jgd->gqij", query, keys, preferred_element_type=jnp.float32) * HD ** (
        -0.5
    )
    places = jnp.arange(slots, dtype=jnp.int32)
    allowed = (
        (seg_rows[:, None] == seg_rows[None, :])
        & (seg_rows[:, None] >= 0)
        & (places[None, :] < places[:, None])
    )
    allowed = allowed | (places[:, None] == places[None, :])
    scores = jnp.where(allowed, scores, -jnp.inf)
    highest = jnp.max(scores, axis=-1, keepdims=True)
    weights = jnp.exp(scores - highest)
    probs = (weights / jnp.sum(weights, axis=-1, keepdims=True)).astype(jnp.bfloat16)
    mixed = jnp.einsum("gqij,jgd->igqd", probs, values, preferred_element_type=jnp.float32)
    mixed = jnp.where((seg_rows >= 0)[:, None, None, None], mixed, 0.0)
    return mixed.reshape(slots, groups * QPK * HD).astype(jnp.bfloat16)


def on_device(
    segments,
    queries,
    keys_values,
    page_table,
    paged_cache,
    residual,
    out_weight,
    norm_gain,
    gate_up_weight,
):
    attended = attention_block(queries, keys_values, segments)
    live_rows = (segments >= 0).astype(jnp.bfloat16)
    every_pair, every_live = (
        lax.all_gather(keys_values, "req", axis=0, tiled=True),
        lax.all_gather(live_rows, "req", axis=0, tiled=True),
    )
    local_pages = paged_cache.shape[0]
    slot_count = every_pair.shape[0]
    token_pages = jnp.repeat(page_table, PAGE, total_repeat_length=slot_count)
    target = token_pages - lax.axis_index("req") * local_pages
    writable = (target >= 0) & (target < local_pages) & (every_live > 0)
    target = jnp.where(writable, target, local_pages)
    offsets = jnp.arange(slot_count, dtype=jnp.int32) % PAGE
    cache_new = paged_cache.at[target, offsets].set(every_pair, mode="drop")
    partial_value = jnp.dot(
        lax.all_gather(attended, "req", axis=0, tiled=True),
        out_weight,
        preferred_element_type=jnp.float32,
    )
    gain_row = norm_gain.astype(jnp.float32)
    stream = residual.astype(jnp.float32) + lax.psum(
        partial_value.astype(jnp.bfloat16), "mdl"
    ).astype(jnp.float32)
    squares = jnp.sum(stream * stream, axis=1)
    totals = lax.psum(squares, "req")
    normed = (stream * lax.rsqrt(totals / D + EPSILON)[:, None] * gain_row[None, :]).astype(
        jnp.bfloat16
    )
    flat_weight = gate_up_weight.reshape(gate_up_weight.shape[0], -1)
    summed = lax.psum_scatter(
        jnp.dot(normed, flat_weight, preferred_element_type=jnp.float32).astype(jnp.bfloat16),
        "req",
        scatter_dimension=0,
        tiled=True,
    ).astype(jnp.float32)
    split_at = summed.shape[1] // 2
    hidden = (jax.nn.silu(summed[:, :split_at]) * summed[:, split_at:]).astype(jnp.bfloat16)
    return (hidden, cache_new)


def solution(mesh):
    placed = (
        P("req"),
        P("req", "mdl"),
        P("req", None, "mdl"),
        P(),
        P("req", None, None, "mdl"),
        P(None, "req"),
        P("mdl", "req"),
        P("req"),
        P("req", None, "mdl"),
    )
    return jax.shard_map(
        on_device,
        mesh=mesh,
        in_specs=placed,
        out_specs=(P("req", "mdl"), P("req", None, None, "mdl")),
        check_vma=False,
    )
```

profile of v0, /device:TPU:0, one launch (start us, length us, event | category | flops | bytes accessed | tf_op | source)
XLA Modules:
  0.0 327.5 jit_solution(5003735953313754061)
XLA Ops:
  7.2 0.9 fusion.16
  8.1 0.7 fusion.15
  8.8 0.8 fusion.13
  9.6 1.2 fusion.21
  10.8 0.1 fusion.8
  10.9 0.2 fusion.4
  11.1 0.1 copy.24
  11.2 0.7 copy.43
  12.0 47.6 %all-gather.2.cloned.1.call-done = bf16[1024,1024]{1,0:T(8,128)(2,1)} async-done(((bf16[64,1024]{1,0:T(8,128)(2,1)}), bf16[1024,1024]{1,0:T(8,128)(2,1)}) %all-gather.2.cloned.1.call-update) | async-done | bytes 2097168 | tf_op jit(solution)/shard_map/all_gather | solution.py:64
  59.6 3.8 %convolution_convert_fusion.1 = bf16[1024,512]{1,0:T(8,128)(2,1)} fusion(bf16[1024,1024]{1,0:T(8,128)(2,1)} %all-gather.2.cloned.1.call-done, bf16[1024,512]{1,0:T(8,128)(2,1)S(1)} %copy-done), kind=kOutput, calls=%fused_computation.5 | convolution fusion | flops 1074266112 | bytes 4194304 | tf_op jit(solution)/shard_map/dot_general | solution.py:63
  63.5 61.8 %all-reduce.3.cloned.1.call-done = bf16[1024,512]{1,0:T(8,128)(2,1)} async-done(((bf16[1024,512]{1,0:T(8,128)(2,1)}), bf16[1024,512]{1,0:T(8,128)(2,1)}) %all-reduce.3.cloned.1.call-update) | async-done | bytes 1048592 | tf_op jit(solution)/shard_map/psum | solution.py:69
  125.3 1.7 multiply_reduce_fusion
  127.1 40.6 %psum.15 = f32[1024]{0:T(1024)S(1)} all-reduce(f32[1024]{0:T(1024)S(1)} %multiply_reduce_fusion), channel_id=1, replica_groups=mesh['req'=16,'mdl'=8] {'req'}, use_global_device_ids=true, to_apply=%region_4.5 | all-reduce | flops 1024 | bytes 8192 | tf_op jit(solution)/shard_map/psum | solution.py:73
  167.7 14.8 %convolution_convert_fusion = bf16[1024,7392]{1,0:T(8,128)(2,1)} fusion(bf16[512,7392]{0,1:T(8,128)(2,1)} %bitcast.142, bf16[1024,512]{1,0:T(8,128)(2,1)S(1)} %copy-done.5, bf16[1024,512]{1,0:T(8,128)(2,1)S(1)} %copy-done.4, f32[512]{0:T(512)S(1)} %convert_element_type.46, f32[1024]{0:T(1024)S(1)} %add_rsqrt_fusion), kind=kOutput, calls=%fused_computation.1 | convolution fusion | flops 7761788928 | bytes 24811520 | tf_op jit(solution)/shard_map/dot_general | solution.py:79
  182.5 0.6 copy-done.11
  183.1 0.6 dynamic-slice.6
  184.3 0.2 dynamic-update-slice.3
  184.5 36.8 %all-reduce = bf16[1024]{0:T(1024)(128)(2,1)S(1)} all-reduce(bf16[1024]{0:T(1024)(128)(2,1)S(1)} %dynamic-update-slice.3), channel_id=1, replica_groups=mesh['req'=16,'mdl'=8] {'req'}, use_global_device_ids=true, to_apply=%add | all-reduce | flops 1024 | bytes 4096
  221.3 0.7 fusion.20
  222.0 0.7 fusion.19
  222.7 0.7 fusion.17
  223.4 0.7 fusion.18
  224.2 0.1 add_add_fusion.1
  224.3 4.4 %compare_select_fusion.2 = (s32[1024,1]{0,1:T(1,128)S(1)}, s32[1024,1]{0,1:T(1,128)S(1)}) fusion(s32[]{:T(128)} %bitcast.73, s32[]{:T(128)} %bitcast.74, s32[]{:T(128)} %bitcast.75, s32[]{:T(128)} %bitcast.76, s32[]{:T(128)} %bitcast.77, s32[]{:T(128)} %bitcast.79, s32[]{:T(128)} %bitcast.78, s32[1024,1]{0,1:T(1,128)S(1)} %bitcast.141, ...), kind=kLoop, calls=%fused_computation.89 | loop fusion | flops 14336 | bytes 16412 | tf_op jit(solution)/shard_map/jit(_take)/gather | solution.py:57
  228.6 0.7 compare_reduce_fusion.56
  229.4 35.7 %compare_select_fusion.8 = s32[1024]{0:T(1024)S(1)} fusion(bf16[1024]{0:T(1024)(128)(2,1)S(1)} %all-reduce, pred[1024]{0:T(1024)(128)(4,1)S(1)} %get-tuple-element.70, pred[1024]{0:T(1024)(128)(4,1)S(1)} %get-tuple-element.69, pred[1024]{0:T(1024)(128)(4,1)S(1)} %get-tuple-element.68, pred[1024]{0:T(1024)(128)(4,1)S(1)} %get-tuple-element.67, ...), kind=kLoop, calls=%fused_computation.97 | loop fusion | flops 79872 | bytes 72968 | tf_op jit(solution)/shard_map/select_n | solution.py:62
  265.1 0.1 multiply_reduce_fusion.1
  265.2 0.1 and_reduce_fusion
  265.3 23.3 %all_gather.11 = bf16[1024,2,128]{2,1,0:T(2,128)(2,1)S(1)} all-gather(bf16[64,2,128]{2,1,0:T(2,128)(2,1)S(1)} %copy-done.6), channel_id=1, replica_groups=mesh['req'=16,'mdl'=8] {'req'}, dimensions={0}, use_global_device_ids=true | all-gather | bytes 557056 | tf_op jit(solution)/shard_map/all_gather | solution.py:52
  288.6 29.9 %scatter_fusion = bf16[128,2,128]{2,1,0:T(2,128)(2,1)S(1)} fusion(bf16[128,2,128]{2,1,0:T(2,128)(2,1)S(1)} %bitcast.134, s32[1024]{0:T(1024)S(1)} %broadcast_select_fusion, bf16[1024,2,128]{2,1,0:T(2,128)(2,1)S(1)} %all_gather.11), kind=kCustom, calls=%fused_computation | custom fusion | bytes 1576960
  318.6 1.3 convert_element_type.49
  319.9 1.1 fusion.7
  (36 shorter events, 0.3 us)
Async XLA Ops:
  7.2 52.4 %copy-start = (bf16[1024,512]{1,0:T(8,128)(2,1)S(1)}, bf16[1024,512]{1,0:T(8,128)(2,1)}, u32[]{:S(2)}) copy-start(bf16[1024,512]{1,0:T(8,128)(2,1)} %param.17) | copy-start | bytes 3145732
  7.2 52.4 %all-gather.2.cloned.1.call-start = ((), (), s32[]{:S(2)}) async-start(), calls=%async_computation.1 | async-start | bytes 2228224 | tf_op jit(solution)/shard_map/all_gather | solution.py:64
  11.9 51.6 %copy-start.8 = (bf16[512]{0:T(512)(128)(2,1)S(1)}, bf16[512]{0:T(512)(128)(2,1)}, u32[]{:S(2)}) copy-start(bf16[512]{0:T(512)(128)(2,1)} %param.18) | copy-start | bytes 3076
  11.9 113.4 %copy-start.4 = (bf16[1024,512]{1,0:T(8,128)(2,1)S(1)}, bf16[1024,512]{1,0:T(8,128)(2,1)}, u32[]{:S(2)}) copy-start(bf16[1024,512]{1,0:T(8,128)(2,1)} %param.16) | copy-start | bytes 3145732
  11.9 113.4 %all-reduce.3.cloned.1.call-start = ((), (), s32[]{:S(2)}) async-start(), calls=%async_computation.2 | async-start | bytes 2097152 | tf_op jit(solution)/shard_map/psum | solution.py:69
  63.4 255.1 %reduce-scatter.2.cloned.1.call-start = ((), (), s32[]{:S(2)}) async-start(), calls=%async_computation.3 | async-start | bytes 16154624 | tf_op jit(solution)/shard_map/reduce_scatter | solution.py:78
  125.3 42.3 %copy-start.5 = (bf16[1024,512]{1,0:T(8,128)(2,1)S(1)}, bf16[1024,512]{1,0:T(8,128)(2,1)}, u32[]{:S(2)}) copy-start(bf16[1024,512]{1,0:T(8,128)(2,1)} %all-reduce.3.cloned.1.call-done) | copy-start | bytes 3145732
  182.4 0.7 copy-start.11
  182.4 38.9 %copy-start.3 = (s32[64]{0:T(128)S(1)}, s32[64]{0:T(128)}, u32[]{:S(2)}) copy-start(s32[64]{0:T(128)} %param.14) | copy-start | bytes 772
  182.4 41.8 %copy-start.7 = (s32[8,128]{1,0:T(8,128)S(1)}, s32[8,128]{1,0:T(8,128)}, u32[]{:S(2)}) copy-start(s32[8,128]{1,0:T(8,128)} %constant.119.clone.1) | copy-start | bytes 12292
  182.4 82.7 %copy-start.10 = (s32[2]{0:T(128)S(1)}, s32[2]{0:T(128)}, u32[]{:S(2)}) copy-start(s32[2]{0:T(128)} %constant.129) | copy-start | bytes 28
  182.4 82.8 %copy-start.9 = (s32[2]{0:T(128)S(1)}, s32[2]{0:T(128)}, u32[]{:S(2)}) copy-start(s32[2]{0:T(128)} %constant.132) | copy-start | bytes 28
  182.4 82.9 %copy-start.6 = (bf16[64,2,128]{2,1,0:T(2,128)(2,1)S(1)}, bf16[64,2,128]{2,1,0:T(2,128)(2,1)}, u32[]{:S(2)}) copy-start(bf16[64,2,128]{2,1,0:T(2,128)(2,1)} %param.13) | copy-start | bytes 98308
  182.4 106.1 %copy-start.2 = (bf16[8,16,2,128]{3,2,1,0:T(2,128)(2,1)S(1)}, bf16[8,16,2,128]{3,2,1,0:T(2,128)(2,1)}, u32[]{:S(2)}) copy-start(bf16[8,16,2,128]{3,2,1,0:T(2,128)(2,1)} %param.15) | copy-start | bytes 196612
  318.5 2.5 copy-start.1
Sparse Core Ops, SparseCore 0:
  12.0 47.5 all-gather.1
  63.6 61.7 all-reduce.2
  182.6 99.0 reduce-scatter.1
where the time goes:
time: 328 us
  waiting for transfers between devices  110 us (34%)
  blocking collectives  101 us (31%)
  other arithmetic  46.8 us (14%)
  local copies, waits for them, and re-layouts  35.9 us (11%)
  matrix products  20 us (6%)
  between operations  14.6 us (4%)
    psum x1, waiting for transfers between devices, on_device(): lax.psum(partial_value.astype(jnp.bfloat16), 'mdl').astype(jnp.float32)  61.8 us
    all_gather x1, waiting for transfers between devices, on_device(): lax.all_gather(attended, 'req', axis=0, tiled=True)  47.6 us
    psum x1, blocking collectives, on_device(): totals = lax.psum(squares, 'req')  40.6 us
    unnamed x1, blocking collectives  36.8 us
    select_n x2, other arithmetic, on_device(): cache_new = paged_cache.at[target, offsets].set(every_pair, mode='drop')  35.7 us
    unnamed x29, local copies, waits for them, and re-layouts  32.1 us
    all_gather x1, blocking collectives, on_device(): lax.all_gather(keys_values, 'req', axis=0, tiled=True)  23.3 us
    dot_general x1, matrix products, on_device(): jnp.dot(normed, flat_weight, preferred_element_type=jnp.float32)  14.8 us
  transfers between devices with their start and end apart: 3, of which 2 were waited for; matrix products, arithmetic and copies ran while one was open for 23% of the time, Pallas kernels for 0%

commit v1 on v0

--- a/solution.py
+++ b/solution.py
@@ -70,7 +70,9 @@
         partial_value.astype(jnp.bfloat16), "mdl"
     ).astype(jnp.float32)
     squares = jnp.sum(stream * stream, axis=1)
-    totals = lax.psum(squares, "req")
+    totals = squares
+    for hop in (1, 2, 4, 8):
+        totals = totals + lax.ppermute(totals, "req", [(dev, dev ^ hop) for dev in range(16)])
     normed = (stream * lax.rsqrt(totals / D + EPSILON)[:, None] * gain_row[None, :]).astype(
         jnp.bfloat16
     )

time: 328 us -> 309 us (0.942)
  blocking collectives: 101 us -> 63.5 us
  starting transfers between devices: 0.12 us -> 9.41 us
  waiting for transfers between devices: 110 us -> 118 us
    psum x1 -> x0, blocking collectives: 40.6 us -> none  [on_device(): totals = lax.psum(squares, 'req')]
    ppermute x0 -> x4, starting transfers between devices: none -> 9.29 us  [on_device(): lax.ppermute(totals, 'req', [(dev, dev ^ hop) for dev in range(16)])]
    ppermute x0 -> x4, waiting for transfers between devices: none -> 8.22 us  [on_device(): lax.ppermute(totals, 'req', [(dev, dev ^ hop) for dev in range(16)])]
    unnamed x1, blocking collectives: 36.8 us -> 41.5 us
  transfers between devices with their start and end apart: 3 -> 7, of which waited for: 2 -> 6; matrix products, arithmetic and copies ran while one was open for 23% -> 24% of each run, Pallas kernels for 0% -> 0%
where the time goes in v1:
time: 309 us; the launch traced here: 308 us
  waiting for transfers between devices  118 us (38%)
  blocking collectives  63.5 us (21%)
  other arithmetic  46.8 us (15%)
  local copies, waits for them, and re-layouts  35.9 us (12%)
  matrix products  20 us (6%)
  between operations  14.6 us (5%)
  starting transfers between devices  9.41 us (3%)
    psum x1, waiting for transfers between devices, on_device(): lax.psum(partial_value.astype(jnp.bfloat16), 'mdl').astype(jnp.float32)  61.8 us
    all_gather x1, waiting for transfers between devices, on_device(): lax.all_gather(attended, 'req', axis=0, tiled=True)  47.6 us
    unnamed x1, blocking collectives  41.5 us
    select_n x2, other arithmetic, on_device(): cache_new = paged_cache.at[target, offsets].set(every_pair, mode='drop')  35.7 us
    unnamed x29, local copies, waits for them, and re-layouts  32.1 us
    all_gather x1, blocking collectives, on_device(): lax.all_gather(keys_values, 'req', axis=0, tiled=True)  22 us
    dot_general x1, matrix products, on_device(): jnp.dot(normed, flat_weight, preferred_element_type=jnp.float32)  14.8 us
    ppermute x4, starting transfers between devices, on_device(): lax.ppermute(totals, 'req', [(dev, dev ^ hop) for dev in range(16)])  9.29 us
  transfers between devices with their start and end apart: 7, of which 6 were waited for; matrix products, arithmetic and copies ran while one was open for 24% of the time, Pallas kernels for 0%

profile of v1, /device:TPU:0, one launch (start us, length us, event | category | flops | bytes accessed | tf_op | source)
XLA Modules:
  0.0 308.0 jit_solution(9133937418498923210)
XLA Ops:
  7.2 0.7 fusion.15
  8.0 0.8 fusion.13
  8.8 0.9 fusion.16
  9.7 1.2 fusion.21
  11.3 0.7 copy.43
  12.0 47.6 %all-gather.2.cloned.1.call-done = bf16[1024,1024]{1,0:T(8,128)(2,1)} async-done(((bf16[64,1024]{1,0:T(8,128)(2,1)}), bf16[1024,1024]{1,0:T(8,128)(2,1)}) %all-gather.2.cloned.1.call-update) | async-done | bytes 2097168 | tf_op jit(solution)/shard_map/all_gather | solution.py:64
  59.7 3.8 %convolution_convert_fusion.1 = bf16[1024,512]{1,0:T(8,128)(2,1)} fusion(bf16[1024,1024]{1,0:T(8,128)(2,1)} %all-gather.2.cloned.1.call-done, bf16[1024,512]{1,0:T(8,128)(2,1)S(1)} %copy-done), kind=kOutput, calls=%fused_computation.5 | convolution fusion | flops 1074266112 | bytes 4194304 | tf_op jit(solution)/shard_map/dot_general | solution.py:63
  63.6 61.8 %all-reduce.3.cloned.1.call-done = bf16[1024,512]{1,0:T(8,128)(2,1)} async-done(((bf16[1024,512]{1,0:T(8,128)(2,1)}), bf16[1024,512]{1,0:T(8,128)(2,1)}) %all-reduce.3.cloned.1.call-update) | async-done | bytes 1048592 | tf_op jit(solution)/shard_map/psum | solution.py:69
  125.4 1.7 multiply_reduce_fusion
  127.1 1.6 collective-permute-start
  128.8 2.1 collective-permute-done
  130.8 3.2 %collective-permute-start.1 = (f32[1024]{0:T(1024)S(1)}, f32[1024]{0:T(1024)S(1)}, u32[]{:S(2)}, u32[]{:S(2)}) collective-permute-start(f32[1024]{0:T(1024)S(1)} %add.108), channel_id=1, source_target_pairs={{0,16},{8,24},{16,0},{24,8},{32,48},{40,56},{48,32},{56,40},{64,80... | collective-permute-start | bytes 12296 | tf_op jit(solution)/shard_map/ppermute | solution.py:75
  134.0 2.0 collective-permute-done.1
  135.9 1.5 collective-permute-start.2
  137.4 2.1 collective-permute-done.2
  139.5 3.0 collective-permute-start.3
  142.6 2.1 collective-permute-done.3
  144.7 14.8 %convolution_convert_fusion = bf16[1024,7392]{1,0:T(8,128)(2,1)} fusion(bf16[512,7392]{0,1:T(8,128)(2,1)} %bitcast.142, bf16[1024,512]{1,0:T(8,128)(2,1)S(1)} %copy-done.5, bf16[1024,512]{1,0:T(8,128)(2,1)S(1)} %copy-done.4, f32[512]{0:T(512)S(1)} %convert_element_type.46, f32[1024]{0:T(1024)S(1)} %add_rsqrt_fusion), kind=kOutput, calls=%fused_computation.1 | convolution fusion | flops 7761788928 | bytes 24811520 | tf_op jit(solution)/shard_map/dot_general | solution.py:81
  159.5 0.6 copy-done.11
  160.1 0.6 dynamic-slice.6
  161.6 41.5 %all-reduce = bf16[1024]{0:T(1024)(128)(2,1)S(1)} all-reduce(bf16[1024]{0:T(1024)(128)(2,1)S(1)} %dynamic-update-slice.3), channel_id=1, replica_groups=mesh['req'=16,'mdl'=8] {'req'}, use_global_device_ids=true, to_apply=%add | all-reduce | flops 1024 | bytes 4096
  203.1 0.7 fusion.20
  203.8 0.7 fusion.19
  204.5 0.7 fusion.17
  205.2 0.7 fusion.18
  206.1 4.4 %compare_select_fusion.2 = (s32[1024,1]{0,1:T(1,128)S(1)}, s32[1024,1]{0,1:T(1,128)S(1)}) fusion(s32[]{:T(128)} %bitcast.73, s32[]{:T(128)} %bitcast.74, s32[]{:T(128)} %bitcast.75, s32[]{:T(128)} %bitcast.76, s32[]{:T(128)} %bitcast.77, s32[]{:T(128)} %bitcast.79, s32[]{:T(128)} %bitcast.78, s32[1024,1]{0,1:T(1,128)S(1)} %bitcast.141, ...), kind=kLoop, calls=%fused_computation.89 | loop fusion | flops 14336 | bytes 16412 | tf_op jit(solution)/shard_map/jit(_take)/gather | solution.py:57
  210.4 0.7 compare_reduce_fusion.56
  211.2 35.7 %compare_select_fusion.8 = s32[1024]{0:T(1024)S(1)} fusion(bf16[1024]{0:T(1024)(128)(2,1)S(1)} %all-reduce, pred[1024]{0:T(1024)(128)(4,1)S(1)} %get-tuple-element.70, pred[1024]{0:T(1024)(128)(4,1)S(1)} %get-tuple-element.69, pred[1024]{0:T(1024)(128)(4,1)S(1)} %get-tuple-element.68, pred[1024]{0:T(1024)(128)(4,1)S(1)} %get-tuple-element.67, ...), kind=kLoop, calls=%fused_computation.97 | loop fusion | flops 79872 | bytes 72968 | tf_op jit(solution)/shard_map/select_n | solution.py:62
  247.1 22.0 %all_gather.11 = bf16[1024,2,128]{2,1,0:T(2,128)(2,1)S(1)} all-gather(bf16[64,2,128]{2,1,0:T(2,128)(2,1)S(1)} %copy-done.6), channel_id=1, replica_groups=mesh['req'=16,'mdl'=8] {'req'}, dimensions={0}, use_global_device_ids=true | all-gather | bytes 557056 | tf_op jit(solution)/shard_map/all_gather | solution.py:52
  269.1 29.9 %scatter_fusion = bf16[128,2,128]{2,1,0:T(2,128)(2,1)S(1)} fusion(bf16[128,2,128]{2,1,0:T(2,128)(2,1)S(1)} %bitcast.134, s32[1024]{0:T(1024)S(1)} %broadcast_select_fusion, bf16[1024,2,128]{2,1,0:T(2,128)(2,1)S(1)} %all_gather.11), kind=kCustom, calls=%fused_computation | custom fusion | bytes 1576960
  299.1 1.3 convert_element_type.49
  300.4 1.1 fusion.7
  (46 shorter events, 1.1 us)
Async XLA Ops:
  7.2 52.5 %copy-start = (bf16[1024,512]{1,0:T(8,128)(2,1)S(1)}, bf16[1024,512]{1,0:T(8,128)(2,1)}, u32[]{:S(2)}) copy-start(bf16[1024,512]{1,0:T(8,128)(2,1)} %param.17) | copy-start | bytes 3145732
  7.2 52.5 %all-gather.2.cloned.1.call-start = ((), (), s32[]{:S(2)}) async-start(), calls=%async_computation.1 | async-start | bytes 2228224 | tf_op jit(solution)/shard_map/all_gather | solution.py:64
  12.0 113.4 %copy-start.4 = (bf16[1024,512]{1,0:T(8,128)(2,1)S(1)}, bf16[1024,512]{1,0:T(8,128)(2,1)}, u32[]{:S(2)}) copy-start(bf16[1024,512]{1,0:T(8,128)(2,1)} %param.16) | copy-start | bytes 3145732
  12.0 113.4 %all-reduce.3.cloned.1.call-start = ((), (), s32[]{:S(2)}) async-start(), calls=%async_computation.2 | async-start | bytes 2097152 | tf_op jit(solution)/shard_map/psum | solution.py:69
  63.5 79.1 %copy-start.8 = (bf16[512]{0:T(512)(128)(2,1)S(1)}, bf16[512]{0:T(512)(128)(2,1)}, u32[]{:S(2)}) copy-start(bf16[512]{0:T(512)(128)(2,1)} %param.18) | copy-start | bytes 3076
  63.5 235.6 %reduce-scatter.2.cloned.1.call-start = ((), (), s32[]{:S(2)}) async-start(), calls=%async_computation.3 | async-start | bytes 16154624 | tf_op jit(solution)/shard_map/reduce_scatter | solution.py:80
  125.4 19.3 %copy-start.5 = (bf16[1024,512]{1,0:T(8,128)(2,1)S(1)}, bf16[1024,512]{1,0:T(8,128)(2,1)}, u32[]{:S(2)}) copy-start(bf16[1024,512]{1,0:T(8,128)(2,1)} %all-reduce.3.cloned.1.call-done) | copy-start | bytes 3145732
  127.1 3.7 %collective-permute-start = (f32[1024]{0:T(1024)S(1)}, f32[1024]{0:T(1024)S(1)}, u32[]{:S(2)}, u32[]{:S(2)}) collective-permute-start(f32[1024]{0:T(1024)S(1)} %multiply_reduce_fusion), channel_id=1, source_target_pairs={{0,8},{8,0},{16,24},{24,16},{32,40},{40,32},{48,56},{56,48},{64,72... | collective-permute-start | bytes 12296 | tf_op jit(solution)/shard_map/ppermute | solution.py:75
  130.8 5.1 %collective-permute-start.1 = (f32[1024]{0:T(1024)S(1)}, f32[1024]{0:T(1024)S(1)}, u32[]{:S(2)}, u32[]{:S(2)}) collective-permute-start(f32[1024]{0:T(1024)S(1)} %add.108), channel_id=1, source_target_pairs={{0,16},{8,24},{16,0},{24,8},{32,48},{40,56},{48,32},{56,40},{64,80... | collective-permute-start | bytes 12296 | tf_op jit(solution)/shard_map/ppermute | solution.py:75
  135.9 3.6 %collective-permute-start.2 = (f32[1024]{0:T(1024)S(1)}, f32[1024]{0:T(1024)S(1)}, u32[]{:S(2)}, u32[]{:S(2)}) collective-permute-start(f32[1024]{0:T(1024)S(1)} %add.109), channel_id=1, source_target_pairs={{0,32},{8,40},{16,48},{24,56},{32,0},{40,8},{48,16},{56,24},{64,96... | collective-permute-start | bytes 12296 | tf_op jit(solution)/shard_map/ppermute | solution.py:75
  139.5 5.1 %collective-permute-start.3 = (f32[1024]{0:T(1024)S(1)}, f32[1024]{0:T(1024)S(1)}, u32[]{:S(2)}, u32[]{:S(2)}) collective-permute-start(f32[1024]{0:T(1024)S(1)} %add.110), channel_id=1, source_target_pairs={{0,64},{8,72},{16,80},{24,88},{32,96},{40,104},{48,112},{56,120},{... | collective-permute-start | bytes 12296 | tf_op jit(solution)/shard_map/ppermute | solution.py:75
  159.4 0.7 copy-start.11
  159.4 43.7 %copy-start.3 = (s32[64]{0:T(128)S(1)}, s32[64]{0:T(128)}, u32[]{:S(2)}) copy-start(s32[64]{0:T(128)} %param.14) | copy-start | bytes 772
  159.4 46.6 %copy-start.7 = (s32[8,128]{1,0:T(8,128)S(1)}, s32[8,128]{1,0:T(8,128)}, u32[]{:S(2)}) copy-start(s32[8,128]{1,0:T(8,128)} %constant.119.clone.1) | copy-start | bytes 12292
  159.4 87.5 %copy-start.10 = (s32[2]{0:T(128)S(1)}, s32[2]{0:T(128)}, u32[]{:S(2)}) copy-start(s32[2]{0:T(128)} %constant.129) | copy-start | bytes 28
  159.4 87.6 %copy-start.9 = (s32[2]{0:T(128)S(1)}, s32[2]{0:T(128)}, u32[]{:S(2)}) copy-start(s32[2]{0:T(128)} %constant.132) | copy-start | bytes 28
  159.4 87.6 %copy-start.6 = (bf16[64,2,128]{2,1,0:T(2,128)(2,1)S(1)}, bf16[64,2,128]{2,1,0:T(2,128)(2,1)}, u32[]{:S(2)}) copy-start(bf16[64,2,128]{2,1,0:T(2,128)(2,1)} %param.13) | copy-start | bytes 98308
  159.5 109.6 %copy-start.2 = (bf16[8,16,2,128]{3,2,1,0:T(2,128)(2,1)S(1)}, bf16[8,16,2,128]{3,2,1,0:T(2,128)(2,1)}, u32[]{:S(2)}) copy-start(bf16[8,16,2,128]{3,2,1,0:T(2,128)(2,1)} %param.15) | copy-start | bytes 196612
  299.0 2.5 copy-start.1
Sparse Core Ops, SparseCore 0:
  12.1 47.5 all-gather.1
  63.6 61.7 all-reduce.2
  159.6 104.7 reduce-scatter.1
